TPU v7x, 256 devices: a whole 4x4x8 slice. The times are simulated.
256 devices in a mesh: seq: 32 (over z_lo, x, core), cam: 4 (over y), tp: 2 (over z_hi).
Axes of the slice: x: 4, y: 4, z: 8 (z_hi: 2, z_lo: 4; z = z_hi * 4 + z_lo), core: 2. Of those that a mesh axis runs over, the one named last changes fastest.
Arguments:
- pixel_feature: bfloat16 [32768, 2048], P(('seq', 'cam'), 'tp'), may hold values from -6 to 6
- depth_score: float32 [32768, 59], P(('seq', 'cam')), may hold values from 0.05 to 5
- depth_bin: int32 [32768, 4], P(('seq', 'cam')), may hold values from 0 to 58
- cell_owner: int32 [131072, 1], P(('seq', 'cam')), may hold values from 0 to 31; in each aligned block of 1024 rows (0 to 1023, 1024 to 2047, ...) at most 64 rows name the same one
- cell_local: int32 [32768, 4], P(('seq', 'cam')), may hold values from 0 to 7
- frame_keep: int32 [64], replicated, may hold values 0 or 1
- norm_gain: float32 [2048], P('tp'), may hold values from 0.1 to 1.9
- w_query: bfloat16 [2048, 2048], P(None, ('cam', 'tp')), may hold values from -1.5 to 1.5
- w_key: bfloat16 [2048, 2048], P(None, ('cam', 'tp')), may hold values from -0.375 to 0.375
- w_value: bfloat16 [2048, 2048], P(None, ('cam', 'tp')), may hold values from -0.125 to 0.125
Outputs:
- attended: bfloat16 [16384, 2048], P('seq', ('cam', 'tp'))
Inputs may be any that keep to these rules, and one draw needn't show every extreme that they name: `cell_owner`: among the 1024 points of one index of seq and cam (aligned blocks of rows), no owner is named more than 64 times, a bound that some block reaches.
All inputs are finite; a program needn't handle non-finite values.
Results may differ from a plain program's by a relative error of at most 0.028.
The roundings to bfloat16 on the way count: a program that leaves them out, or rounds other values in their place, can miss the bound.
Values may be sent and summed in bfloat16 or wider, within the bound.
A program may use at most 64 MiB of HBM per device.

v0:
```python
import jax
import jax.numpy as jnp
from jax import lax
from jax.sharding import PartitionSpec as P

D = 2048
HD = 128
CELL_DEV = 8
epsilon = 1e-05
block_rows = 512


def attend(state, query, query_start, keys, values, key_start, frame_keep):
    frames = frame_keep.shape[0]
    frame_query = (query_start + jnp.arange(query.shape[0], dtype=jnp.int32)) % frames
    frame_key = (key_start + jnp.arange(keys.shape[0], dtype=jnp.int32)) % frames
    frame_list = jnp.arange(frames, dtype=jnp.int32)
    kept = jnp.sum(
        jnp.where(frame_key[:, None] == frame_list[None, :], frame_keep[None, :], 0), axis=1
    )
    allowed = (frame_key[None, :] <= frame_query[:, None]) & (
        (kept[None, :] > 0) | (frame_key[None, :] == frame_query[:, None])
    )
    scores = jnp.einsum("qhd,khd->hqk", query, keys, preferred_element_type=jnp.float32) * (
        1.0 / HD**0.5
    )
    accum, peak, total = state
    new_peak = jnp.maximum(peak, jnp.max(jnp.where(allowed[None], scores, -1e30), axis=2))
    factor = jnp.exp(peak - new_peak)
    expo = jnp.where(allowed[None], jnp.exp(scores - new_peak[:, :, None]), 0.0)
    mixed = jnp.einsum(
        "hqk,khd->hqd", expo.astype(jnp.bfloat16), values, preferred_element_type=jnp.float32
    )
    return (accum * factor[:, :, None] + mixed, new_peak, total * factor + jnp.sum(expo, axis=2))


def local(
    pixel_feature,
    depth_score,
    depth_bin,
    cell_owner,
    cell_local,
    frame_keep,
    norm_gain,
    w_query,
    w_key,
    w_value,
):
    pixels, half = pixel_feature.shape
    keep_count = depth_bin.shape[1]
    points = pixels * keep_count
    seq_count = lax.axis_size("seq")
    seq_index = lax.axis_index("seq")
    frames = frame_keep.shape[0]
    frames_dev = frames // seq_count
    tokens_dev = CELL_DEV * frames
    capacity = 2 * points // seq_count
    prob = depth_score / jnp.sum(depth_score, axis=1, keepdims=True)
    bins = jnp.arange(depth_score.shape[1], dtype=jnp.int32)
    picked = jnp.sum(
        jnp.where(depth_bin[:, :, None] == bins[None, None, :], prob[:, None, :], 0.0), axis=2
    )
    weight = picked.astype(jnp.bfloat16)
    point_index = jnp.arange(points, dtype=jnp.int32).reshape(pixels, keep_count)
    local_frame = point_index // (points // frames_dev)
    owner = cell_owner[:, 0].reshape(pixels, keep_count)
    owner_flat = owner.reshape(points)
    hits = (owner_flat[:, None] == jnp.arange(seq_count, dtype=jnp.int32)[None, :]).astype(
        jnp.int32
    )
    rank = jnp.sum(jnp.cumsum(hits, axis=0) * hits, axis=1) - 1
    slot = owner_flat * capacity + rank
    point_rows = jnp.repeat(pixel_feature, keep_count, axis=0)
    send_rows = jnp.zeros((seq_count * capacity, half), jnp.bfloat16).at[slot].set(point_rows)
    send_rows = send_rows.reshape(seq_count, capacity, half)
    frame_global = seq_index * frames_dev + local_frame
    describe = jnp.stack(
        [
            weight.reshape(points),
            cell_local.reshape(points).astype(jnp.bfloat16),
            frame_global.reshape(points).astype(jnp.bfloat16),
        ],
        axis=0,
    )
    send_meta = jnp.zeros((3, seq_count * capacity), jnp.bfloat16).at[:, slot].set(describe)
    send_meta = send_meta.reshape(3, seq_count, capacity).transpose(1, 0, 2)
    got_rows, got_meta = (
        lax.all_to_all(send_rows, "seq", split_axis=0, concat_axis=0, tiled=True),
        lax.all_to_all(send_meta, "seq", split_axis=0, concat_axis=0, tiled=True),
    )
    target = (
        got_meta[:, 1, :].astype(jnp.float32) * frames + got_meta[:, 2, :].astype(jnp.float32)
    ).reshape(-1)
    token_ids = jnp.arange(tokens_dev, dtype=jnp.float32)
    mixing = jnp.where(
        token_ids[:, None] == target[None, :], got_meta[:, 0, :].reshape(-1)[None, :], 0
    )
    pooled = jnp.dot(mixing, got_rows.reshape(-1, half), preferred_element_type=jnp.float32)
    bev = lax.psum(pooled, "cam")
    squares = lax.psum(jnp.sum(bev * bev, axis=1), "tp")
    normed = (bev * lax.rsqrt(squares[:, None] / D + epsilon) * norm_gain[None, :]).astype(
        jnp.bfloat16
    )
    width = w_query.shape[1]
    heads_dev = width // HD
    piece = lax.all_gather(normed, "tp", axis=1, tiled=True)
    query_sum = jnp.dot(piece, w_query, preferred_element_type=jnp.float32)
    key_sum = jnp.dot(piece, w_key, preferred_element_type=jnp.float32)
    value_sum = jnp.dot(piece, w_value, preferred_element_type=jnp.float32)
    query = query_sum.astype(jnp.bfloat16).reshape(tokens_dev, heads_dev, HD)
    keys = key_sum.astype(jnp.bfloat16).reshape(tokens_dev, heads_dev, HD)
    values = value_sum.astype(jnp.bfloat16).reshape(tokens_dev, heads_dev, HD)
    query_start = seq_index * tokens_dev
    start_state = (
        jnp.zeros((heads_dev, tokens_dev, HD), jnp.float32),
        jnp.full((heads_dev, tokens_dev), -1e30, jnp.float32),
        jnp.zeros((heads_dev, tokens_dev), jnp.float32),
    )
    piece_keys = lax.all_gather(keys, "seq", axis=0, tiled=True)
    piece_values = lax.all_gather(values, "seq", axis=0, tiled=True)
    count = piece_keys.shape[0]

    def one_block(index, inner):
        block_keys = lax.dynamic_slice_in_dim(piece_keys, index * block_rows, block_rows, 0)
        block_values = lax.dynamic_slice_in_dim(piece_values, index * block_rows, block_rows, 0)
        return attend(
            inner, query, query_start, block_keys, block_values, index * block_rows, frame_keep
        )

    accum, peak, total = lax.fori_loop(0, count // block_rows, one_block, start_state)
    result = accum / total[:, :, None]
    return result.transpose(1, 0, 2).reshape(tokens_dev, width).astype(jnp.bfloat16)


def solution(mesh):
    return jax.shard_map(
        local,
        mesh=mesh,
        in_specs=(
            P(("seq", "cam"), "tp"),
            P(("seq", "cam"), None),
            P(("seq", "cam"), None),
            P(("seq", "cam"), None),
            P(("seq", "cam"), None),
            P(),
            P("tp"),
            P(None, ("cam", "tp")),
            P(None, ("cam", "tp")),
            P(None, ("cam", "tp")),
        ),
        out_specs=P("seq", ("cam", "tp")),
        check_vma=False,
    )
```

profile of v0, /device:TPU:1, one launch (start us, length us, event | category | flops | bytes accessed | tf_op | source)
XLA Modules:
  0.0 587.0 jit_solution(16973022452448787255)
XLA Ops:
  11.1 9.0 %reduce-window.6 = s32[32,8,128]{2,1,0:T(8,128)S(1)} reduce-window(s32[32,8,128]{2,1,0:T(8,128)S(1)} %fusion.34, s32[]{:T(128)} %constant.143.clone.1), window={size=1x1x128 pad=0_0x0_0x127_0}, to_apply=%region_0.0 | reduce-window | flops 4161536 | bytes 262148 | tf_op jit(solution)/shard_map/reduce-window
  22.4 3.3 scatter_custom_fusion
  26.7 10.0 %all-to-all-start = ((bf16[32,3,64]{2,1,0:T(4,128)(2,1)}), bf16[32,3,64]{2,1,0:T(4,128)(2,1)S(1)}, u32[]{:S(2)}, u32[]{:S(2)}) async-start(bf16[32,3,64]{2,1,0:T(4,128)(2,1)} %bitcast.8), calls=%async_computation | async-start | bytes 65536 | tf_op jit(solution)/shard_map/all_to_all | solution.py:89
  38.4 2.1 reshape.333
  40.4 8.6 %scatter_custom_fusion.1 = bf16[2048,1024]{1,0:T(8,128)(2,1)} fusion(s32[1024]{0:T(1024)S(1)} %bitcast.76, bf16[1024,1024]{1,0:T(8,128)(2,1)} %reshape.333, bf16[]{:T(256)} %constant.146.clone.1), kind=kCustom, calls=%fused_computation.44 | custom fusion | bytes 4194816 | tf_op jit(solution)/shard_map/scatter | solution.py:74
  49.0 7.8 %all-to-all-start.1 = ((bf16[32,64,1024]{2,1,0:T(8,128)(2,1)}), bf16[32,64,1024]{2,1,0:T(8,128)(2,1)}, u32[]{:S(2)}, u32[]{:S(2)}) async-start(bf16[32,64,1024]{2,1,0:T(8,128)(2,1)} %bitcast.65), calls=%async_computation.1 | async-start | bytes 8388608 | tf_op jit(solution)/shard_map/all_to_all | solution.py:88
  57.2 92.7 %all-to-all-done.1 = bf16[32,64,1024]{2,1,0:T(8,128)(2,1)} async-done(((bf16[32,64,1024]{2,1,0:T(8,128)(2,1)}), bf16[32,64,1024]{2,1,0:T(8,128)(2,1)}, u32[]{:S(2)}, u32[]{:S(2)}) %all-to-all-start.1) | async-done | bytes 4194336 | tf_op jit(solution)/shard_map/all_to_all | solution.py:88
  149.9 5.9 fusion.22
  155.8 64.2 %all-reduce.2.cloned.1.call-done = f32[512,1024]{1,0:T(8,128)} async-done(((f32[512,1024]{1,0:T(8,128)}), f32[512,1024]{1,0:T(8,128)}) %all-reduce.2.cloned.1.call-update) | async-done | bytes 2097168 | tf_op jit(solution)/shard_map/psum | solution.py:99
  221.9 7.8 %psum.15 = f32[512]{0:T(512)S(1)} all-reduce(f32[512]{0:T(512)S(1)} %multiply_reduce_fusion), channel_id=1, replica_groups=mesh['seq'=32,'cam'=4,'tp'=2] {'tp'}, use_global_device_ids=true, to_apply=%region_9.10 | all-reduce | flops 512 | bytes 4096 | tf_op jit(solution)/shard_map/psum | solution.py:100
  231.2 65.9 %all-gather.4.cloned.1.call-done = bf16[512,2048]{1,0:T(8,128)(2,1)} async-done(((bf16[512,1024]{1,0:T(8,128)(2,1)}), bf16[512,2048]{1,0:T(8,128)(2,1)}) %all-gather.4.cloned.1.call-update) | async-done | bytes 2097168 | tf_op jit(solution)/shard_map/all_gather | solution.py:106
  297.2 2.5 convolution_convert_fusion
  300.6 2.0 convolution_convert_fusion.2
  303.5 2.6 convolution_convert_fusion.1
  306.3 59.7 %all-gather.8.cloned.1.call-done = bf16[16384,2,128]{2,0,1:T(8,128)(2,1)} async-done(((bf16[512,2,128]{2,0,1:T(8,128)(2,1)}), bf16[16384,2,128]{2,0,1:T(8,128)(2,1)}) %all-gather.8.cloned.1.call-update) | async-done | bytes 8388624 | tf_op jit(solution)/shard_map/all_gather | solution.py:120
  366.0 69.0 %all-gather.6.cloned.1.call-done = bf16[16384,2,128]{2,0,1:T(8,128)(2,1)} async-done(((bf16[512,2,128]{2,0,1:T(8,128)(2,1)}), bf16[16384,2,128]{2,0,1:T(8,128)(2,1)}) %all-gather.6.cloned.1.call-update) | async-done | bytes 8388624 | tf_op jit(solution)/shard_map/all_gather | solution.py:119
  435.0 144.5 %while.20 = (s32[]{:T(128)}, f32[2,512,128]{2,1,0:T(8,128)S(1)}, f32[2,512]{1,0:T(2,128)S(1)}, f32[2,512]{1,0:T(2,128)S(1)}, s32[]{:T(128)}, /*index=5*/s32[64]{...) while((s32[]{:T(128)}, f32[2,512,128]{2,1,0:T(8,128)S(1)}, ...), condition=%wide.region_14.15_spmd.clone, body=%wide.region_10.14_spmd.clone.sunk | while | flops 275760128 | bytes 9256399 | solution.py:130
  437.5 2.0 convolution_add_fusion.2
  442.0 2.0 convolution_add_fusion.2
  446.5 2.0 convolution_add_fusion.2
  451.0 2.0 convolution_add_fusion.2
  455.5 2.0 convolution_add_fusion.2
  460.1 2.0 convolution_add_fusion.2
  464.6 2.0 convolution_add_fusion.2
  469.1 2.0 convolution_add_fusion.2
  473.6 2.0 convolution_add_fusion.2
  478.1 2.0 convolution_add_fusion.2
  482.7 2.0 convolution_add_fusion.2
  487.2 2.0 convolution_add_fusion.2
  491.7 2.0 convolution_add_fusion.2
  496.2 2.0 convolution_add_fusion.2
  500.7 2.0 convolution_add_fusion.2
  505.2 2.0 convolution_add_fusion.2
  509.8 2.0 convolution_add_fusion.2
  514.3 2.0 convolution_add_fusion.2
  518.8 2.0 convolution_add_fusion.2
  523.3 2.0 convolution_add_fusion.2
  527.8 2.0 convolution_add_fusion.2
  532.4 2.0 convolution_add_fusion.2
  536.9 2.0 convolution_add_fusion.2
  541.4 2.0 convolution_add_fusion.2
  545.9 2.0 convolution_add_fusion.2
  550.4 2.0 convolution_add_fusion.2
  554.9 2.0 convolution_add_fusion.2
  559.5 2.0 convolution_add_fusion.2
  564.0 2.0 convolution_add_fusion.2
  568.5 2.0 convolution_add_fusion.2
  573.0 2.0 convolution_add_fusion.2
  (347 shorter events, 97.8 us)
Async XLA Ops:
  6.5 290.6 %copy-start = (bf16[2048,256]{1,0:T(8,128)(2,1)S(1)}, bf16[2048,256]{1,0:T(8,128)(2,1)}, u32[]{:S(2)}) copy-start(bf16[2048,256]{1,0:T(8,128)(2,1)} %param.21) | copy-start | bytes 3145732
  26.7 22.4 %all-to-all-start = ((bf16[32,3,64]{2,1,0:T(4,128)(2,1)}), bf16[32,3,64]{2,1,0:T(4,128)(2,1)S(1)}, u32[]{:S(2)}, u32[]{:S(2)}) async-start(bf16[32,3,64]{2,1,0:T(4,128)(2,1)} %bitcast.8), calls=%async_computation | async-start | bytes 65536 | tf_op jit(solution)/shard_map/all_to_all | solution.py:89
  49.0 100.9 %all-to-all-start.1 = ((bf16[32,64,1024]{2,1,0:T(8,128)(2,1)}), bf16[32,64,1024]{2,1,0:T(8,128)(2,1)}, u32[]{:S(2)}, u32[]{:S(2)}) async-start(bf16[32,64,1024]{2,1,0:T(8,128)(2,1)} %bitcast.65), calls=%async_computation.1 | async-start | bytes 8388608 | tf_op jit(solution)/shard_map/all_to_all | solution.py:88
  56.8 163.2 %all-reduce.2.cloned.1.call-start = ((), (), s32[]{:S(2)}) async-start(), calls=%async_computation.2 | async-start | bytes 4194304 | tf_op jit(solution)/shard_map/psum | solution.py:99
  155.7 74.0 %copy-start.3 = (f32[1024]{0:T(1024)S(1)}, f32[1024]{0:T(1024)}, u32[]{:S(2)}) copy-start(f32[1024]{0:T(1024)} %param.18) | copy-start | bytes 12292
  155.8 141.4 %all-gather.4.cloned.1.call-start = ((), (), s32[]{:S(2)}) async-start(), calls=%async_computation.3 | async-start | bytes 3145728 | tf_op jit(solution)/shard_map/all_gather | solution.py:106
  220.0 9.7 %copy-start.1 = (f32[512,1024]{1,0:T(8,128)S(1)}, f32[512,1024]{1,0:T(8,128)}, u32[]{:S(2)}) copy-start(f32[512,1024]{1,0:T(8,128)} %all-reduce.2.cloned.1.call-done) | copy-start | bytes 6291460
  231.0 135.0 %all-gather.8.cloned.1.call-start = ((), (), s32[]{:S(2)}) async-start(), calls=%async_computation.5 | async-start | bytes 8650752 | tf_op jit(solution)/shard_map/all_gather | solution.py:120
  297.2 3.4 copy-start.4
  300.5 134.4 %all-gather.6.cloned.1.call-start = ((), (), s32[]{:S(2)}) async-start(), calls=%async_computation.4 | async-start | bytes 8650752 | tf_op jit(solution)/shard_map/all_gather | solution.py:119
  303.5 131.5 %copy-start.2 = (s32[64]{0:T(128)S(1)}, s32[64]{0:T(128)}, u32[]{:S(2)}) copy-start(s32[64]{0:T(128)} %param.17) | copy-start | bytes 772
Sparse Core Ops, SparseCore 0:
  155.9 64.0 all-reduce.1
  231.1 66.0 all-gather.3
  300.7 65.2 all-gather.7
  367.7 67.1 all-gather.5
where the time goes:
time: 590 us; the launch traced here: 587 us
  waiting for transfers between devices  352 us (60%)
  matrix products  124 us (21%)
  other arithmetic  50.4 us (9%)
  local copies, waits for them, and re-layouts  19.9 us (3%)
  starting transfers between devices  18.1 us (3%)
  between operations  13.3 us (2%)
  blocking collectives  7.76 us (1%)
    all_to_all x1, waiting for transfers between devices, local(): lax.all_to_all(send_rows, 'seq', split_axis=0, concat_axis=0, tiled=True)  92.7 us
    all_gather x1, waiting for transfers between devices, local(): piece_keys = lax.all_gather(keys, 'seq', axis=0, tiled=True)  69 us
    all_gather x1, waiting for transfers between devices, local(): piece = lax.all_gather(normed, 'tp', axis=1, tiled=True)  65.9 us
    psum x1, waiting for transfers between devices, local(): bev = lax.psum(pooled, 'cam')  64.2 us
    dot_general x32, matrix products, attend(): jnp.einsum('hqk,khd->hqd', expo.astype(jnp.bfloat16), values, preferred_e...  62.6 us
    all_gather x1, waiting for transfers between devices, local(): piece_values = lax.all_gather(values, 'seq', axis=0, tiled=True)  59.7 us
    dot_general x32, matrix products, attend(): jnp.einsum('qhd,khd->hqk', query, keys, preferred_element_type=jnp.float32)  48.2 us
    reduce_sum x32, other arithmetic, attend(): jnp.sum(expo, axis=2)  15.9 us
  transfers between devices with their start and end apart: 6, of which 5 were waited for; matrix products, arithmetic and copies ran while one was open for 3% of the time, Pallas kernels for 0%

commit v1 on v0

--- a/solution.py
+++ b/solution.py
@@ -96,7 +96,8 @@
         token_ids[:, None] == target[None, :], got_meta[:, 0, :].reshape(-1)[None, :], 0
     )
     pooled = jnp.dot(mixing, got_rows.reshape(-1, half), preferred_element_type=jnp.float32)
-    bev = lax.psum(pooled, "cam")
+    parts = lax.all_gather(pooled, "cam", axis=0, tiled=False)
+    bev = parts.sum(axis=0)
     squares = lax.psum(jnp.sum(bev * bev, axis=1), "tp")
     normed = (bev * lax.rsqrt(squares[:, None] / D + epsilon) * norm_gain[None, :]).astype(
         jnp.bfloat16

time: 590 us -> 615 us (1.042)
  waiting for transfers between devices: 352 us -> 375 us
    all_gather x0 -> x1, waiting for transfers between devices: none -> 85.8 us  [local(): parts = lax.all_gather(pooled, 'cam', axis=0, tiled=False)]
    psum x1 -> x0, waiting for transfers between devices: 64.2 us -> none  [local(): bev = lax.psum(pooled, 'cam')]
where the time goes in v1:
time: 615 us; the launch traced here: 613 us
  waiting for transfers between devices  375 us (61%)
  matrix products  124 us (20%)
  other arithmetic  53.2 us (9%)
  local copies, waits for them, and re-layouts  19.9 us (3%)
  starting transfers between devices  18.1 us (3%)
  between operations  13.3 us (2%)
  blocking collectives  7.76 us (1%)
    all_to_all x1, waiting for transfers between devices, local(): lax.all_to_all(send_rows, 'seq', split_axis=0, concat_axis=0, tiled=True)  92.7 us
    all_gather x1, waiting for transfers between devices, local(): parts = lax.all_gather(pooled, 'cam', axis=0, tiled=False)  85.8 us
    all_gather x1, waiting for transfers between devices, local(): piece_keys = lax.all_gather(keys, 'seq', axis=0, tiled=True)  69 us
    all_gather x1, waiting for transfers between devices, local(): piece = lax.all_gather(normed, 'tp', axis=1, tiled=True)  67.3 us
    dot_general x32, matrix products, attend(): jnp.einsum('hqk,khd->hqd', expo.astype(jnp.bfloat16), values, preferred_e...  62.6 us
    all_gather x1, waiting for transfers between devices, local(): piece_values = lax.all_gather(values, 'seq', axis=0, tiled=True)  59.7 us
    dot_general x32, matrix products, attend(): jnp.einsum('qhd,khd->hqk', query, keys, preferred_element_type=jnp.float32)  48.2 us
    reduce_sum x32, other arithmetic, attend(): jnp.sum(expo, axis=2)  15.9 us
  transfers between devices with their start and end apart: 6, of which 5 were waited for; matrix products, arithmetic and copies ran while one was open for 3% of the time, Pallas kernels for 0%

profile of v1, /device:TPU:1, one launch (start us, length us, event | category | flops | bytes accessed | tf_op | source)
XLA Modules:
  0.0 612.9 jit_solution(9555049285022522366)
XLA Ops:
  11.1 9.0 %reduce-window.6 = s32[32,8,128]{2,1,0:T(8,128)S(1)} reduce-window(s32[32,8,128]{2,1,0:T(8,128)S(1)} %fusion.34, s32[]{:T(128)} %constant.143.clone.1), window={size=1x1x128 pad=0_0x0_0x127_0}, to_apply=%region_0.0 | reduce-window | flops 4161536 | bytes 262148 | tf_op jit(solution)/shard_map/reduce-window
  22.4 3.3 scatter_custom_fusion
  26.7 10.0 %all-to-all-start = ((bf16[32,3,64]{2,1,0:T(4,128)(2,1)}), bf16[32,3,64]{2,1,0:T(4,128)(2,1)S(1)}, u32[]{:S(2)}, u32[]{:S(2)}) async-start(bf16[32,3,64]{2,1,0:T(4,128)(2,1)} %bitcast.8), calls=%async_computation | async-start | bytes 65536 | tf_op jit(solution)/shard_map/all_to_all | solution.py:89
  38.4 2.1 reshape.333
  40.4 8.6 %scatter_custom_fusion.1 = bf16[2048,1024]{1,0:T(8,128)(2,1)} fusion(s32[1024]{0:T(1024)S(1)} %bitcast.78, bf16[1024,1024]{1,0:T(8,128)(2,1)} %reshape.333, bf16[]{:T(256)} %constant.146.clone.1), kind=kCustom, calls=%fused_computation.44 | custom fusion | bytes 4194816 | tf_op jit(solution)/shard_map/scatter | solution.py:74
  49.0 7.8 %all-to-all-start.1 = ((bf16[32,64,1024]{2,1,0:T(8,128)(2,1)}), bf16[32,64,1024]{2,1,0:T(8,128)(2,1)}, u32[]{:S(2)}, u32[]{:S(2)}) async-start(bf16[32,64,1024]{2,1,0:T(8,128)(2,1)} %bitcast.66), calls=%async_computation.1 | async-start | bytes 8388608 | tf_op jit(solution)/shard_map/all_to_all | solution.py:88
  57.2 92.7 %all-to-all-done.1 = bf16[32,64,1024]{2,1,0:T(8,128)(2,1)} async-done(((bf16[32,64,1024]{2,1,0:T(8,128)(2,1)}), bf16[32,64,1024]{2,1,0:T(8,128)(2,1)}, u32[]{:S(2)}, u32[]{:S(2)}) %all-to-all-start.1) | async-done | bytes 4194336 | tf_op jit(solution)/shard_map/all_to_all | solution.py:88
  149.9 5.9 fusion.22
  156.1 85.8 %all-gather.12.cloned.1.call-done = f32[2048,1024]{1,0:T(8,128)} async-done(((f32[512,1024]{1,0:T(8,128)}), f32[2048,1024]{1,0:T(8,128)}) %all-gather.12.cloned.1.call-update) | async-done | bytes 8388624 | tf_op jit(solution)/shard_map/all_gather | solution.py:99
  241.9 4.6 reduce_sum.80
  246.7 7.8 %psum.7 = f32[512]{0:T(512)S(1)} all-reduce(f32[512]{0:T(512)S(1)} %multiply_reduce_fusion), channel_id=1, replica_groups=mesh['seq'=32,'cam'=4,'tp'=2] {'tp'}, use_global_device_ids=true, to_apply=%region_9.10 | all-reduce | flops 512 | bytes 4096 | tf_op jit(solution)/shard_map/psum | solution.py:101
  255.8 67.3 %all-gather.6.cloned.1.call-done = bf16[512,2048]{1,0:T(8,128)(2,1)} async-done(((bf16[512,1024]{1,0:T(8,128)(2,1)}), bf16[512,2048]{1,0:T(8,128)(2,1)}) %all-gather.6.cloned.1.call-update) | async-done | bytes 2097168 | tf_op jit(solution)/shard_map/all_gather | solution.py:107
  323.1 2.5 convolution_convert_fusion
  326.5 2.0 convolution_convert_fusion.2
  329.4 2.6 convolution_convert_fusion.1
  332.2 59.7 %all-gather.10.cloned.1.call-done = bf16[16384,2,128]{2,0,1:T(8,128)(2,1)} async-done(((bf16[512,2,128]{2,0,1:T(8,128)(2,1)}), bf16[16384,2,128]{2,0,1:T(8,128)(2,1)}) %all-gather.10.cloned.1.call-update) | async-done | bytes 8388624 | tf_op jit(solution)/shard_map/all_gather | solution.py:121
  391.9 69.0 %all-gather.8.cloned.1.call-done = bf16[16384,2,128]{2,0,1:T(8,128)(2,1)} async-done(((bf16[512,2,128]{2,0,1:T(8,128)(2,1)}), bf16[16384,2,128]{2,0,1:T(8,128)(2,1)}) %all-gather.8.cloned.1.call-update) | async-done | bytes 8388624 | tf_op jit(solution)/shard_map/all_gather | solution.py:120
  460.9 144.5 %while.20 = (s32[]{:T(128)}, f32[2,512,128]{2,1,0:T(8,128)S(1)}, f32[2,512]{1,0:T(2,128)S(1)}, f32[2,512]{1,0:T(2,128)S(1)}, s32[]{:T(128)}, /*index=5*/s32[64]{...) while((s32[]{:T(128)}, f32[2,512,128]{2,1,0:T(8,128)S(1)}, ...), condition=%wide.region_14.15_spmd.clone, body=%wide.region_10.14_spmd.clone.sunk | while | flops 275760128 | bytes 9256399 | solution.py:131
  463.4 2.0 convolution_add_fusion.2
  467.9 2.0 convolution_add_fusion.2
  472.4 2.0 convolution_add_fusion.2
  476.9 2.0 convolution_add_fusion.2
  481.4 2.0 convolution_add_fusion.2
  486.0 2.0 convolution_add_fusion.2
  490.5 2.0 convolution_add_fusion.2
  495.0 2.0 convolution_add_fusion.2
  499.5 2.0 convolution_add_fusion.2
  504.0 2.0 convolution_add_fusion.2
  508.5 2.0 convolution_add_fusion.2
  513.1 2.0 convolution_add_fusion.2
  517.6 2.0 convolution_add_fusion.2
  522.1 2.0 convolution_add_fusion.2
  526.6 2.0 convolution_add_fusion.2
  531.1 2.0 convolution_add_fusion.2
  535.7 2.0 convolution_add_fusion.2
  540.2 2.0 convolution_add_fusion.2
  544.7 2.0 convolution_add_fusion.2
  549.2 2.0 convolution_add_fusion.2
  553.7 2.0 convolution_add_fusion.2
  558.2 2.0 convolution_add_fusion.2
  562.8 2.0 convolution_add_fusion.2
  567.3 2.0 convolution_add_fusion.2
  571.8 2.0 convolution_add_fusion.2
  576.3 2.0 convolution_add_fusion.2
  580.8 2.0 convolution_add_fusion.2
  585.4 2.0 convolution_add_fusion.2
  589.9 2.0 convolution_add_fusion.2
  594.4 2.0 convolution_add_fusion.2
  (346 shorter events, 98.1 us)
Async XLA Ops:
  6.5 316.5 %copy-start = (bf16[2048,256]{1,0:T(8,128)(2,1)S(1)}, bf16[2048,256]{1,0:T(8,128)(2,1)}, u32[]{:S(2)}) copy-start(bf16[2048,256]{1,0:T(8,128)(2,1)} %param.21) | copy-start | bytes 3145732
  26.7 22.4 %all-to-all-start = ((bf16[32,3,64]{2,1,0:T(4,128)(2,1)}), bf16[32,3,64]{2,1,0:T(4,128)(2,1)S(1)}, u32[]{:S(2)}, u32[]{:S(2)}) async-start(bf16[32,3,64]{2,1,0:T(4,128)(2,1)} %bitcast.8), calls=%async_computation | async-start | bytes 65536 | tf_op jit(solution)/shard_map/all_to_all | solution.py:89
  49.0 100.9 %all-to-all-start.1 = ((bf16[32,64,1024]{2,1,0:T(8,128)(2,1)}), bf16[32,64,1024]{2,1,0:T(8,128)(2,1)}, u32[]{:S(2)}, u32[]{:S(2)}) async-start(bf16[32,64,1024]{2,1,0:T(8,128)(2,1)} %bitcast.66), calls=%async_computation.1 | async-start | bytes 8388608 | tf_op jit(solution)/shard_map/all_to_all | solution.py:88
  56.8 185.1 %all-gather.12.cloned.1.call-start = ((), (), s32[]{:S(2)}) async-start(), calls=%async_computation.5 | async-start | bytes 10485760 | tf_op jit(solution)/shard_map/all_gather | solution.py:99
  155.8 167.2 %all-gather.6.cloned.1.call-start = ((), (), s32[]{:S(2)}) async-start(), calls=%async_computation.2 | async-start | bytes 3145728 | tf_op jit(solution)/shard_map/all_gather | solution.py:107
  246.5 8.0 %copy-start.2 = (f32[1024]{0:T(1024)S(1)}, f32[1024]{0:T(1024)}, u32[]{:S(2)}) copy-start(f32[1024]{0:T(1024)} %param.18) | copy-start | bytes 12292
  255.7 136.2 %all-gather.10.cloned.1.call-start = ((), (), s32[]{:S(2)}) async-start(), calls=%async_computation.4 | async-start | bytes 8650752 | tf_op jit(solution)/shard_map/all_gather | solution.py:121
  323.1 3.4 copy-start.3
  326.4 134.4 %all-gather.8.cloned.1.call-start = ((), (), s32[]{:S(2)}) async-start(), calls=%async_computation.3 | async-start | bytes 8650752 | tf_op jit(solution)/shard_map/all_gather | solution.py:120
  329.4 131.5 %copy-start.1 = (s32[64]{0:T(128)S(1)}, s32[64]{0:T(128)}, u32[]{:S(2)}) copy-start(s32[64]{0:T(128)} %param.17) | copy-start | bytes 772
Sparse Core Ops, SparseCore 0:
  156.0 85.8 all-gather.11
  255.8 67.1 all-gather.5
  326.6 65.2 all-gather.9
  393.6 67.1 all-gather.7
